TPU v7x, 256 devices: a whole 4x4x8 slice. The times are simulated.
256 devices in a mesh: member: 16 (over z, y_hi), lat: 4 (over x), lon: 4 (over y_lo, core).
Axes of the slice: x: 4, y: 4 (y_hi: 2, y_lo: 2; y = y_hi * 2 + y_lo), z: 8, core: 2. Of those that a mesh axis runs over, the one named last changes fastest.
Arguments:
- ensemble: bfloat16 [32, 16, 64, 256], P('member', 'lat', 'lon'), may hold values from -12 to 12
- norm_gain: float32 [256], replicated, may hold values from 0.5 to 1.5
- project_weight: bfloat16 [256, 768], replicated, may hold values from -0.375 to 0.375
- output_weight: bfloat16 [256, 256], replicated, may hold values from -0.375 to 0.375
- conv_kernel: bfloat16 [3, 3, 256, 256], replicated, may hold values from -0.125 to 0.125
- cotangent: bfloat16 [32, 16, 64, 256], P('member', 'lat', 'lon'), may hold values from -6 to 6
Outputs:
- result: bfloat16 [32, 16, 64, 256], P('member', 'lat', 'lon')
- grad_ensemble: bfloat16 [32, 16, 64, 256], P('member', 'lat', 'lon')
All inputs are finite; a program needn't handle non-finite values.
Results may differ from a plain program's by a relative error of at most 0.018.
Values may be sent and summed in bfloat16 or wider, within the bound.
A program may use at most 64 MiB of HBM per device.

v0:
```python
import math
import jax
import jax.numpy as jnp
from jax import lax
from jax.sharding import PartitionSpec as P

HEAD_COUNT = 8
FLOOR = 0.5
EPSILON = 1e-06


def padded_2(block, sides, width, periodic):
    for axis, dim in sides:
        count = lax.axis_size(axis)
        forward = [(i, i + 1) for i in range(count - 1)]
        if periodic:
            forward.append((count - 1, 0))
        backward = [(target, source) for source, target in forward]
        low = lax.ppermute(
            lax.slice_in_dim(block, block.shape[dim] - width, None, axis=dim), axis, forward
        )
        high = lax.ppermute(lax.slice_in_dim(block, 0, width, axis=dim), axis, backward)
        block = jnp.concatenate([low, block, high], axis=dim)
    return block


def row_norm(values, gain_vec):
    mean_sq = jnp.mean(values * values, axis=-1, keepdims=True)
    return values * lax.rsqrt(mean_sq + EPSILON) * gain_vec


def head_norm(values, head_count):
    shaped = values.reshape(values.shape[:-1] + (head_count, values.shape[-1] // head_count))
    mean_sq = jnp.mean(shaped * shaped, axis=-1, keepdims=True)
    return (shaped * lax.rsqrt(jnp.maximum(mean_sq, FLOOR))).reshape(values.shape)


def split_heads(values, head_count):
    return values.reshape(values.shape[:-1] + (head_count, values.shape[-1] // head_count))


def head_pullback(raw_rows, grad_rows):
    _, pullback = jax.vjp(lambda t: head_norm(t, HEAD_COUNT), raw_rows.astype(jnp.float32))
    return pullback(grad_rows)[0]


def pad_field(field_in):
    widened = padded_2(field_in, (("lon", 2),), 1, True)
    return padded_2(widened, (("lat", 1),), 1, False)


def conv_taps(padded, kernel, lat_n, lon_n, adjoint):
    running = None
    for row_off in range(3):
        for col_off in range(3):
            if adjoint:
                window = padded[
                    :, 2 - row_off : 2 - row_off + lat_n, 2 - col_off : 2 - col_off + lon_n
                ]
                summand = jnp.einsum(
                    "mabc,dc->mabd",
                    window,
                    kernel[row_off, col_off],
                    preferred_element_type=jnp.float32,
                )
            else:
                window = padded[:, row_off : row_off + lat_n, col_off : col_off + lon_n]
                summand = jnp.einsum(
                    "mabc,cd->mabd",
                    window,
                    kernel[row_off, col_off],
                    preferred_element_type=jnp.float32,
                )
            running = summand if running is None else running + summand
    return running


def per_device(ensemble, norm_gain, project_weight, output_weight, conv_kernel, cotangent):
    mem_dev, lat_dev, lon_dev, channels = ensemble.shape
    cell_count = lat_dev * lon_dev
    score_scale = 1.0 / math.sqrt(channels // HEAD_COUNT)
    inputs = ensemble.reshape(mem_dev, cell_count, channels).astype(jnp.float32)
    normed = row_norm(inputs, norm_gain).astype(jnp.bfloat16)
    query_raw = jnp.dot(
        normed, project_weight[:, :channels], preferred_element_type=jnp.float32
    ).astype(jnp.bfloat16)
    gathered = jnp.dot(
        lax.all_gather(normed, "member", axis=0, tiled=True),
        project_weight[:, channels:],
        preferred_element_type=jnp.float32,
    ).astype(jnp.bfloat16)
    own_rows = lax.dynamic_slice_in_dim(gathered, lax.axis_index("member") * mem_dev, mem_dev, 0)
    key_raw = own_rows[..., :channels]
    key_rows = head_norm(gathered[..., :channels].astype(jnp.float32), HEAD_COUNT).astype(
        jnp.bfloat16
    )
    value_rows = gathered[..., channels:]
    queries = head_norm(query_raw.astype(jnp.float32), HEAD_COUNT).astype(jnp.bfloat16)
    query_heads = split_heads(queries, HEAD_COUNT)
    key_heads = split_heads(key_rows, HEAD_COUNT)
    value_heads = split_heads(value_rows, HEAD_COUNT)
    scores = (
        jnp.einsum("mphd,nphd->mnhp", query_heads, key_heads, preferred_element_type=jnp.float32)
        * score_scale
    )
    expd = jnp.exp(scores)
    soft = expd / jnp.sum(expd, axis=1, keepdims=True)
    rounded = soft.astype(jnp.bfloat16)
    mixed_out = jnp.einsum(
        "mnhp,nphd->mphd", rounded, value_heads, preferred_element_type=jnp.float32
    )
    mixed_out = mixed_out.reshape(query_raw.shape).astype(jnp.bfloat16)
    updated = (
        inputs + jnp.dot(mixed_out, output_weight, preferred_element_type=jnp.float32)
    ).astype(jnp.bfloat16)
    field_up = updated.reshape(mem_dev, lat_dev, lon_dev, channels)
    result = field_up.astype(jnp.float32) + conv_taps(
        pad_field(field_up), conv_kernel, lat_dev, lon_dev, False
    )
    result = result.astype(jnp.bfloat16)
    grad_field = cotangent.astype(jnp.float32) + conv_taps(
        pad_field(cotangent), conv_kernel, lat_dev, lon_dev, True
    )
    grad_rows = grad_field.reshape(mem_dev, cell_count, channels)
    grad_mixed = jnp.einsum(
        "mpc,dc->mpd",
        grad_rows.astype(jnp.bfloat16),
        output_weight,
        preferred_element_type=jnp.float32,
    )
    grad_mixed = grad_mixed.astype(jnp.bfloat16)
    grad_heads = split_heads(grad_mixed, HEAD_COUNT)
    dprob = jnp.einsum(
        "mphd,nphd->mnhp", grad_heads, value_heads, preferred_element_type=jnp.float32
    )
    dscore = (soft * (dprob - jnp.sum(soft * dprob, axis=1, keepdims=True))).astype(jnp.bfloat16)
    query_grad = (
        jnp.einsum("mnhp,nphd->mphd", dscore, key_heads, preferred_element_type=jnp.float32)
        * score_scale
    )
    query_grad = query_grad.reshape(query_raw.shape)
    row_count = mem_dev * lax.axis_size("member")
    key_part = (
        jnp.einsum("mnhp,mphd->nphd", dscore, query_heads, preferred_element_type=jnp.float32)
        * score_scale
    )
    value_part = jnp.einsum(
        "mnhp,mphd->nphd", rounded, grad_heads, preferred_element_type=jnp.float32
    )
    summed = lax.psum_scatter(
        jnp.concatenate(
            [
                key_part.reshape(row_count, cell_count, channels),
                value_part.reshape(row_count, cell_count, channels),
            ],
            axis=-1,
        ).astype(jnp.bfloat16),
        "member",
        scatter_dimension=0,
        tiled=True,
    ).astype(jnp.float32)
    key_grad = summed[..., :channels]
    value_grad = summed[..., channels:]
    grad_query_raw = head_pullback(query_raw, query_grad)
    grad_key_raw = head_pullback(key_raw, key_grad)
    grad_proj = jnp.concatenate([grad_query_raw, grad_key_raw, value_grad], axis=-1).astype(
        jnp.bfloat16
    )
    grad_normed = jnp.einsum(
        "mpe,ce->mpc", grad_proj, project_weight, preferred_element_type=jnp.float32
    )
    _, pull_norm = jax.vjp(lambda t: row_norm(t, norm_gain), inputs)
    grad_inputs = pull_norm(grad_normed)[0]
    grad_ensemble = (
        (grad_rows + grad_inputs).astype(jnp.bfloat16).reshape(mem_dev, lat_dev, lon_dev, channels)
    )
    return (result, grad_ensemble)


def solution(mesh):
    in_specs = (
        P("member", "lat", "lon", None),
        P(),
        P(),
        P(),
        P(),
        P("member", "lat", "lon", None),
    )
    out_specs = (P("member", "lat", "lon", None), P("member", "lat", "lon", None))
    return jax.shard_map(
        per_device, mesh=mesh, in_specs=in_specs, out_specs=out_specs, check_vma=False
    )
```

profile of v0, /device:TPU:1, one launch (start us, length us, event | category | flops | bytes accessed | tf_op | source)
XLA Modules:
  0.0 408.8 jit_solution(2294606689336277992)
XLA Ops:
  8.1 2.8 collective-permute-start.4
  11.5 0.9 multiply_reduce_fusion.2
  12.6 1.6 multiply_convert_fusion.2
  14.2 1.1 fusion.50
  15.3 1.1 fusion.18
  17.8 0.9 copy.161
  18.8 1.3 collective-permute-start.6
  20.1 4.0 collective-permute-start.7
  26.9 0.9 copy.154
  27.9 0.9 copy.164
  28.8 62.1 %all-gather.2.cloned.1.call-done = bf16[32,64,256]{2,1,0:T(8,128)(2,1)} async-done(((bf16[2,64,256]{2,1,0:T(8,128)(2,1)}), bf16[32,64,256]{2,1,0:T(8,128)(2,1)}) %all-gather.2.cloned.1.call-update) | async-done | bytes 1048592 | tf_op jit(solution)/shard_map/all_gather | solution.py:88
  90.9 1.9 convolution_convert_fusion.1
  92.8 1.2 slice.190
  94.5 1.6 convert_multiply_fusion.1
  96.1 2.0 copy.138
  98.1 6.5 %copy.153 = bf16[32,64,8,32]{3,0,1,2:T(8,128)(2,1)} copy(bf16[32,64,8,32]{1,3,2,0:T(8,128)(2,1)S(1)} %bitcast.179) | data formatting | bytes 2097152 | tf_op jit(solution)/shard_map/reshape | solution.py:39
  104.6 5.3 %fusion.115 = f32[8,64,32,2]{2,3,1,0:T(2,128)} fusion(bf16[32,64,8,32]{3,0,1,2:T(8,128)(2,1)} %copy.153, bf16[2,64,8,32]{3,0,1,2:T(2,128)(2,1)} %copy.154), kind=kOutput, calls=%fused_computation.175 | convolution fusion | flops 2097152 | bytes 1245184 | tf_op jit(solution)/shard_map/mphd,nphd->mnhp/dot_general | solution.py:133
  109.9 2.0 copy.155
  111.9 3.8 copy.139
  115.7 3.1 bitcast_reduce_fusion
  118.8 2.2 mul.208
  121.0 3.8 copy.140
  124.8 3.2 fusion
  128.0 2.7 copy.141
  130.8 7.5 %copy.145 = bf16[32,64,8,32]{3,0,1,2:T(8,128)(2,1)} copy(bf16[32,64,8,32]{1,3,2,0:T(8,128)(2,1)} %bitcast.181) | data formatting | bytes 2097152 | tf_op jit(solution)/shard_map/reshape | solution.py:39
  138.3 5.3 %fusion.114 = f32[8,64,32,2]{2,3,1,0:T(2,128)} fusion(bf16[32,64,8,32]{3,0,1,2:T(8,128)(2,1)} %copy.145, bf16[2,64,8,32]{3,0,1,2:T(2,128)(2,1)} %copy.146), kind=kOutput, calls=%fused_computation.174 | convolution fusion | flops 2097152 | bytes 1245184 | tf_op jit(solution)/shard_map/mphd,nphd->mnhp/dot_general | solution.py:103
  143.6 1.9 copy.147
  145.5 1.0 bitcast_reduce_fusion.3
  146.5 1.1 fusion.23
  147.6 1.8 fusion.25
  149.4 1.9 copy.157
  151.3 4.5 %multiply_convert_fusion = bf16[64,8,32,32]{3,2,1,0:T(8,128)(2,1)} fusion(bf16[2,64,8,32]{3,0,2,1:T(2,128)(2,1)} %copy.161, bf16[2,32,8,64]{1,0,2,3:T(2,128)(2,1)} %copy.157), kind=kOutput, calls=%fused_computation | convolution fusion | flops 3145728 | bytes 1179648 | tf_op jit(solution)/shard_map/mnhp,mphd->nphd/dot_general | solution.py:144
  155.8 4.9 %copy.167 = bf16[32,64,256]{2,1,0:T(8,128)(2,1)} copy(bf16[32,64,256]{0,2,1:T(8,128)(2,1)} %bitcast.183) | data formatting | bytes 2097152 | tf_op jit(solution)/shard_map/reshape | solution.py:153
  160.7 1.9 copy.149
  162.6 4.3 %convolution_convert_fusion = bf16[64,8,32,32]{3,2,1,0:T(8,128)(2,1)} fusion(bf16[2,64,8,32]{3,0,2,1:T(2,128)(2,1)} %copy.164, bf16[2,32,8,64]{1,0,2,3:T(2,128)(2,1)} %copy.149), kind=kOutput, calls=%fused_computation.2 | convolution fusion | flops 2621440 | bytes 1179648 | tf_op jit(solution)/shard_map/mnhp,mphd->nphd/dot_general | solution.py:147
  166.9 4.9 %copy.168 = bf16[32,64,256]{2,1,0:T(8,128)(2,1)} copy(bf16[32,64,256]{0,2,1:T(8,128)(2,1)} %bitcast.184) | data formatting | bytes 2097152 | tf_op jit(solution)/shard_map/reshape | solution.py:154
  171.8 3.1 pad_maximum_fusion
  174.9 7.8 %copy.156 = bf16[32,64,8,32]{3,0,2,1:T(8,128)(2,1)} copy(bf16[32,64,8,32]{1,3,2,0:T(8,128)(2,1)} %bitcast.182) | data formatting | bytes 2097152 | tf_op jit(solution)/shard_map/reshape | solution.py:39
  182.7 6.8 %copy.148 = bf16[32,64,8,32]{3,0,2,1:T(8,128)(2,1)} copy(bf16[32,64,8,32]{1,3,2,0:T(8,128)(2,1)S(1)} %bitcast.180) | data formatting | bytes 2097152 | tf_op jit(solution)/shard_map/reshape | solution.py:39
  189.5 3.4 fusion.116
  193.9 3.4 fusion.1
  197.5 182.2 %reduce-scatter.2.cloned.1.call-done = bf16[2,64,512]{2,1,0:T(8,128)(2,1)} async-done(((bf16[32,64,512]{2,1,0:T(8,128)(2,1)}), bf16[2,64,512]{2,1,0:T(8,128)(2,1)}) %reduce-scatter.2.cloned.1.call-update) | async-done | bytes 131088 | tf_op jit(solution)/shard_map/reduce_scatter | solution.py:150
  379.8 0.9 convert_multiply_fusion.4
  382.9 6.3 %collective-permute-start = (bf16[2,4,1,256]{3,2,1,0:T(2,128)(2,1)S(1)}, bf16[2,4,1,256]{3,2,1,0:T(2,128)(2,1)S(1)}, u32[]{:S(2)}, u32[]{:S(2)}) collective-permute-start(bf16[2,4,1,256]{3,2,1,0:T(2,128)(2,1)S(1)} %get-tuple-element.16), channel_id=1, source_target_pairs={{0,1},{1,2},{2,3},{3,0},{4,5},{5,6},{6,7},{7,4},{8,9},{9,10},{10,1... | collective-permute-start | bytes 12296 | tf_op jit(solution)/shard_map/ppermute | solution.py:19
  390.1 2.2 collective-permute-done.1
  392.3 3.2 collective-permute-start.2
  395.5 1.3 collective-permute-start.3
  397.0 3.1 collective-permute-done.3
  (95 shorter events, 12.5 us)
Async XLA Ops:
  7.2 19.4 %copy-start = (bf16[256,256]{1,0:T(8,128)(2,1)S(1)}, bf16[256,256]{1,0:T(8,128)(2,1)}, u32[]{:S(2)}) copy-start(bf16[256,256]{1,0:T(8,128)(2,1)} %param.9) | copy-start | bytes 393220
  7.2 11.6 %copy-start.5 = (bf16[2,4,16,256]{3,2,1,0:T(8,128)(2,1)S(1)}, bf16[2,4,16,256]{3,2,1,0:T(8,128)(2,1)}, u32[]{:S(2)}) copy-start(bf16[2,4,16,256]{3,2,1,0:T(8,128)(2,1)} %param.11) | copy-start | bytes 196612
  7.2 16.9 %copy-start.2 = (bf16[3,3,256,256]{3,2,1,0:T(8,128)(2,1)S(1)}, bf16[3,3,256,256]{3,2,1,0:T(8,128)(2,1)}, u32[]{:S(2)}) copy-start(bf16[3,3,256,256]{3,2,1,0:T(8,128)(2,1)} %param.10) | copy-start | bytes 3538948
  7.2 83.7 %all-gather.2.cloned.1.call-start = ((), (), s32[]{:S(2)}) async-start(), calls=%async_computation.1 | async-start | bytes 1114112 | tf_op jit(solution)/shard_map/all_gather | solution.py:88
  8.1 10.7 %collective-permute-start.4 = (bf16[2,4,1,256]{3,2,1,0:T(2,128)(2,1)S(1)}, bf16[2,4,1,256]{3,2,1,0:T(2,128)(2,1)S(1)}, u32[]{:S(2)}, u32[]{:S(2)}) collective-permute-start(bf16[2,4,1,256]{3,2,1,0:T(2,128)(2,1)S(1)} %get-tuple-element.18), channel_id=1, source_target_pairs={{0,1},{1,2},{2,3},{3,0},{4,5},{5,6},{6,7},{7,4},{8,9},{9,10},{10,1... | collective-permute-start | bytes 12296 | tf_op jit(solution)/shard_map/ppermute | solution.py:19
  10.9 7.9 %collective-permute-start.5 = (bf16[2,4,1,256]{3,2,1,0:T(2,128)(2,1)S(1)}, bf16[2,4,1,256]{3,2,1,0:T(2,128)(2,1)S(1)}, u32[]{:S(2)}, u32[]{:S(2)}) collective-permute-start(bf16[2,4,1,256]{3,2,1,0:T(2,128)(2,1)S(1)} %get-tuple-element.19), channel_id=1, source_target_pairs={{1,0},{2,1},{3,2},{0,3},{5,4},{6,5},{7,6},{4,7},{9,8},{10,9},{11,1... | collective-permute-start | bytes 12296 | tf_op jit(solution)/shard_map/ppermute | solution.py:22
  14.2 365.6 %reduce-scatter.2.cloned.1.call-start = ((), (), s32[]{:S(2)}) async-start(), calls=%async_computation.2 | async-start | bytes 2228224 | tf_op jit(solution)/shard_map/reduce_scatter | solution.py:150
  16.6 9.3 %copy-start.3 = (f32[2,64,256]{1,2,0:T(8,128)}, f32[2,64,256]{1,2,0:T(8,128)S(1)}, u32[]{:S(2)}) copy-start(f32[2,64,256]{1,2,0:T(8,128)S(1)} %copy.142) | copy-start | bytes 393220
  18.8 5.5 %collective-permute-start.6 = (bf16[2,1,18,256]{3,2,1,0:T(8,128)(2,1)S(1)}, bf16[2,1,18,256]{3,2,1,0:T(8,128)(2,1)S(1)}, u32[]{:S(2)}, u32[]{:S(2)}) collective-permute-start(bf16[2,1,18,256]{3,2,1,0:T(8,128)(2,1)S(1)} %get-tuple-element.14), channel_id=1, source_target_pairs={{4,0},{8,4},{12,8},{5,1},{9,5},{13,9},{6,2},{10,6},{14,10},{7,3},{... | collective-permute-start | bytes 55304 | tf_op jit(solution)/shard_map/ppermute | solution.py:22
  20.1 4.9 %collective-permute-start.7 = (bf16[2,1,18,256]{3,2,1,0:T(8,128)(2,1)S(1)}, bf16[2,1,18,256]{3,2,1,0:T(8,128)(2,1)S(1)}, u32[]{:S(2)}, u32[]{:S(2)}) collective-permute-start(bf16[2,1,18,256]{3,2,1,0:T(8,128)(2,1)S(1)} %get-tuple-element.15), channel_id=1, source_target_pairs={{0,4},{4,8},{8,12},{1,5},{5,9},{9,13},{2,6},{6,10},{10,14},{3,7},{... | collective-permute-start | bytes 55304 | tf_op jit(solution)/shard_map/ppermute | solution.py:19
  25.5 65.4 %copy-start.8 = (bf16[256,768]{1,0:T(8,128)(2,1)S(1)}, bf16[256,768]{1,0:T(8,128)(2,1)}, u32[]{:S(2)}) copy-start(bf16[256,768]{1,0:T(8,128)(2,1)} %param.8) | copy-start | bytes 1179652
  92.8 1.7 copy-start.1
  189.5 3.8 copy-start.4
  192.9 1.0 copy-start.6
  197.3 185.0 %copy-start.7 = (bf16[2,4,16,256]{3,2,1,0:T(8,128)(2,1)S(1)}, bf16[2,4,16,256]{3,2,1,0:T(8,128)(2,1)}, u32[]{:S(2)}) copy-start(bf16[2,4,16,256]{3,2,1,0:T(8,128)(2,1)} %param.6) | copy-start | bytes 196612
  197.3 185.0 %copy-start.9 = (bf16[256,768]{1,0:T(8,128)(2,1)S(1)}, bf16[256,768]{1,0:T(8,128)(2,1)}, u32[]{:S(2)}) copy-start(bf16[256,768]{1,0:T(8,128)(2,1)} %param.8) | copy-start | bytes 1179652
  197.3 185.0 %copy-start.11 = (f32[256]{0:T(256)S(1)}, f32[256]{0:T(256)}, u32[]{:S(2)}) copy-start(f32[256]{0:T(256)} %param.7) | copy-start | bytes 3076
  379.8 1.6 copy-start.10
  379.8 2.5 slice-start
  382.9 7.2 %collective-permute-start = (bf16[2,4,1,256]{3,2,1,0:T(2,128)(2,1)S(1)}, bf16[2,4,1,256]{3,2,1,0:T(2,128)(2,1)S(1)}, u32[]{:S(2)}, u32[]{:S(2)}) collective-permute-start(bf16[2,4,1,256]{3,2,1,0:T(2,128)(2,1)S(1)} %get-tuple-element.16), channel_id=1, source_target_pairs={{0,1},{1,2},{2,3},{3,0},{4,5},{5,6},{6,7},{7,4},{8,9},{9,10},{10,1... | collective-permute-start | bytes 12296 | tf_op jit(solution)/shard_map/ppermute | solution.py:19
  389.2 3.1 collective-permute-start.1
  392.3 4.7 %collective-permute-start.2 = (bf16[2,1,18,256]{3,2,1,0:T(8,128)(2,1)S(1)}, bf16[2,1,18,256]{3,2,1,0:T(8,128)(2,1)S(1)}, u32[]{:S(2)}, u32[]{:S(2)}) collective-permute-start(bf16[2,1,18,256]{3,2,1,0:T(8,128)(2,1)S(1)} %get-tuple-element.10), channel_id=1, source_target_pairs={{0,4},{4,8},{8,12},{1,5},{5,9},{9,13},{2,6},{6,10},{10,14},{3,7},{... | collective-permute-start | bytes 55304 | tf_op jit(solution)/shard_map/ppermute | solution.py:19
  395.5 4.6 %collective-permute-start.3 = (bf16[2,1,18,256]{3,2,1,0:T(8,128)(2,1)S(1)}, bf16[2,1,18,256]{3,2,1,0:T(8,128)(2,1)S(1)}, u32[]{:S(2)}, u32[]{:S(2)}) collective-permute-start(bf16[2,1,18,256]{3,2,1,0:T(8,128)(2,1)S(1)} %get-tuple-element.11), channel_id=1, source_target_pairs={{4,0},{8,4},{12,8},{5,1},{9,5},{13,9},{6,2},{10,6},{14,10},{7,3},{... | collective-permute-start | bytes 55304 | tf_op jit(solution)/shard_map/ppermute | solution.py:22
Sparse Core Ops, SparseCore 0:
  14.3 76.5 all-gather.1
  175.0 204.7 reduce-scatter.1
where the time goes:
time: 410 us; the launch traced here: 409 us
  waiting for transfers between devices  250 us (61%)
  local copies, waits for them, and re-layouts  69.1 us (17%)
  matrix products  34.8 us (8%)
  other arithmetic  20.5 us (5%)
  starting transfers between devices  19.5 us (5%)
  between operations  14.7 us (4%)
    reduce_scatter x1, waiting for transfers between devices, per_device(): lax.psum_scatter(jnp.concatenate([key_part.reshape(row_count, cell_count,...  182 us
    all_gather x1, waiting for transfers between devices, per_device(): lax.all_gather(normed, 'member', axis=0, tiled=True)  62.1 us
    reshape x8, local copies, waits for them, and re-layouts, split_heads(): values.reshape(values.shape[:-1] + (head_count, values.shape[-1] // head_...  32.2 us
    ppermute x4, starting transfers between devices, padded_2(): lax.ppermute(lax.slice_in_dim(block, block.shape[dim] - width, None, axis...  16.2 us
  transfers between devices with their start and end apart: 10, of which 5 were waited for; matrix products, arithmetic and copies ran while one was open for 8% of the time, Pallas kernels for 0%

commit v1 on v0

--- a/solution.py
+++ b/solution.py
@@ -85,7 +85,9 @@
         normed, project_weight[:, :channels], preferred_element_type=jnp.float32
     ).astype(jnp.bfloat16)
     gathered = jnp.dot(
-        lax.all_gather(normed, "member", axis=0, tiled=True),
+        jnp.concatenate(
+            lax.all_to_all(jnp.stack([normed] * lax.axis_size("member")), "member", 0, 0), axis=0
+        ),
         project_weight[:, channels:],
         preferred_element_type=jnp.float32,
     ).astype(jnp.bfloat16)

time: 410 us -> 368 us (0.90)
  waiting for transfers between devices: 250 us -> 199 us
  starting transfers between devices: 19.5 us -> 29.4 us
    all_gather x1 -> x0, waiting for transfers between devices: 62.1 us -> none  [per_device(): lax.all_gather(normed, 'member', axis=0, tiled=True)]
    all_to_all x0 -> x1, waiting for transfers between devices: none -> 13 us  [per_device(): lax.all_to_all(jnp.stack([normed] * lax.axis_size('member')), 'member', 0...]
    all_to_all x0 -> x1, starting transfers between devices: none -> 10 us  [per_device(): lax.all_to_all(jnp.stack([normed] * lax.axis_size('member')), 'member', 0...]
  transfers between devices with their start and end apart: 10 -> 10, of which waited for: 5 -> 5; matrix products, arithmetic and copies ran while one was open for 8% -> 9% of each run, Pallas kernels for 0% -> 0%
where the time goes in v1:
time: 368 us; the launch traced here: 366 us
  waiting for transfers between devices  199 us (54%)
  local copies, waits for them, and re-layouts  70.1 us (19%)
  matrix products  33.5 us (9%)
  starting transfers between devices  29.4 us (8%)
  other arithmetic  19.8 us (5%)
  between operations  14.7 us (4%)
    reduce_scatter x1, waiting for transfers between devices, per_device(): lax.psum_scatter(jnp.concatenate([key_part.reshape(row_count, cell_count,...  180 us
    reshape x8, local copies, waits for them, and re-layouts, split_heads(): values.reshape(values.shape[:-1] + (head_count, values.shape[-1] // head_...  32.3 us
    ppermute x4, starting transfers between devices, padded_2(): lax.ppermute(lax.slice_in_dim(block, block.shape[dim] - width, None, axis...  16.1 us
    all_to_all x1, waiting for transfers between devices, per_device(): lax.all_to_all(jnp.stack([normed] * lax.axis_size('member')), 'member', 0...  13 us
    all_to_all x1, starting transfers between devices, per_device(): lax.all_to_all(jnp.stack([normed] * lax.axis_size('member')), 'member', 0...  10 us
  transfers between devices with their start and end apart: 10, of which 5 were waited for; matrix products, arithmetic and copies ran while one was open for 9% of the time, Pallas kernels for 0%

profile of v1, /device:TPU:1, one launch (start us, length us, event | category | flops | bytes accessed | tf_op | source)
XLA Modules:
  0.0 366.3 jit_solution(11104704746102220765)
XLA Ops:
  8.1 2.8 collective-permute-start.4
  11.5 0.9 multiply_reduce_fusion.2
  12.5 0.9 multiply_convert_fusion.2
  13.5 1.1 stack.2
  14.5 10.0 %all-to-all-start = ((bf16[16,2,64,256]{3,2,1,0:T(8,128)(2,1)}), bf16[16,2,64,256]{3,2,1,0:T(8,128)(2,1)S(1)}, u32[]{:S(2)}, u32[]{:S(2)}) async-start(bf16[16,2,64,256]{3,2,1,0:T(8,128)(2,1)} %stack.2), calls=%async_computation | async-start | bytes 2097152 | tf_op jit(solution)/shard_map/all_to_all | solution.py:89
  24.8 1.1 fusion.18
  27.3 0.9 copy.161
  28.3 1.3 collective-permute-start.6
  29.6 4.0 %collective-permute-start.7 = (bf16[2,1,18,256]{3,2,1,0:T(8,128)(2,1)S(1)}, bf16[2,1,18,256]{3,2,1,0:T(8,128)(2,1)S(1)}, u32[]{:S(2)}, u32[]{:S(2)}) collective-permute-start(bf16[2,1,18,256]{3,2,1,0:T(8,128)(2,1)S(1)} %get-tuple-element.15), channel_id=1, source_target_pairs={{0,4},{4,8},{8,12},{1,5},{5,9},{9,13},{2,6},{6,10},{10,14},{3,7},{... | collective-permute-start | bytes 55304 | tf_op jit(solution)/shard_map/ppermute | solution.py:19
  36.3 0.9 copy.154
  37.3 0.9 copy.164
  38.2 13.0 %all-to-all-done = bf16[16,2,64,256]{3,2,1,0:T(8,128)(2,1)S(1)} async-done(((bf16[16,2,64,256]{3,2,1,0:T(8,128)(2,1)}), bf16[16,2,64,256]{3,2,1,0:T(8,128)(2,1)S(1)}, u32[]{:S(2)}, u32[]{:S(2)}) %all-to-all-start) | async-done | bytes 1048608 | tf_op jit(solution)/shard_map/all_to_all | solution.py:89
  51.3 1.6 convolution_convert_fusion.1
  52.9 1.2 slice.190
  54.6 1.6 convert_multiply_fusion.1
  56.1 2.0 copy.138
  58.2 6.5 %copy.153 = bf16[32,64,8,32]{3,0,1,2:T(8,128)(2,1)} copy(bf16[32,64,8,32]{1,3,2,0:T(8,128)(2,1)S(1)} %bitcast.180) | data formatting | bytes 2097152 | tf_op jit(solution)/shard_map/reshape | solution.py:39
  64.6 5.3 %fusion.115 = f32[8,64,32,2]{2,3,1,0:T(2,128)} fusion(bf16[32,64,8,32]{3,0,1,2:T(8,128)(2,1)} %copy.153, bf16[2,64,8,32]{3,0,1,2:T(2,128)(2,1)} %copy.154), kind=kOutput, calls=%fused_computation.175 | convolution fusion | flops 2097152 | bytes 1245184 | tf_op jit(solution)/shard_map/mphd,nphd->mnhp/dot_general | solution.py:135
  69.9 2.0 copy.155
  71.9 3.8 %copy.139 = f32[32,64,256]{1,2,0:T(8,128)} copy(f32[32,64,256]{2,1,0:T(8,128)} %convert_multiply_fusion.1) | data formatting | bytes 4194304 | tf_op jit(solution)/shard_map/mul | solution.py:34
  75.7 3.1 bitcast_reduce_fusion
  78.8 2.2 mul.212
  81.0 3.8 %copy.140 = f32[32,64,256]{2,1,0:T(8,128)} copy(f32[32,64,256]{1,2,0:T(8,128)} %bitcast.186) | data formatting | bytes 4194304 | tf_op jit(solution)/shard_map/mul | solution.py:35
  84.9 3.2 fusion
  88.1 2.7 copy.141
  90.8 7.5 %copy.145 = bf16[32,64,8,32]{3,0,1,2:T(8,128)(2,1)} copy(bf16[32,64,8,32]{1,3,2,0:T(8,128)(2,1)} %bitcast.182) | data formatting | bytes 2097152 | tf_op jit(solution)/shard_map/reshape | solution.py:39
  98.3 5.3 %fusion.114 = f32[8,64,32,2]{2,3,1,0:T(2,128)} fusion(bf16[32,64,8,32]{3,0,1,2:T(8,128)(2,1)} %copy.145, bf16[2,64,8,32]{3,0,1,2:T(2,128)(2,1)} %copy.146), kind=kOutput, calls=%fused_computation.174 | convolution fusion | flops 2097152 | bytes 1245184 | tf_op jit(solution)/shard_map/mphd,nphd->mnhp/dot_general | solution.py:105
  103.6 1.9 copy.147
  105.5 1.0 bitcast_reduce_fusion.3
  106.5 1.1 fusion.23
  107.6 1.8 fusion.25
  109.5 1.9 copy.157
  111.4 4.5 %multiply_convert_fusion = bf16[64,8,32,32]{3,2,1,0:T(8,128)(2,1)} fusion(bf16[2,64,8,32]{3,0,2,1:T(2,128)(2,1)} %copy.161, bf16[2,32,8,64]{1,0,2,3:T(2,128)(2,1)} %copy.157), kind=kOutput, calls=%fused_computation | convolution fusion | flops 3145728 | bytes 1179648 | tf_op jit(solution)/shard_map/mnhp,mphd->nphd/dot_general | solution.py:146
  115.9 4.9 %copy.167 = bf16[32,64,256]{2,1,0:T(8,128)(2,1)} copy(bf16[32,64,256]{0,2,1:T(8,128)(2,1)} %bitcast.184) | data formatting | bytes 2097152 | tf_op jit(solution)/shard_map/reshape | solution.py:155
  120.7 1.9 copy.149
  122.6 4.3 %convolution_convert_fusion = bf16[64,8,32,32]{3,2,1,0:T(8,128)(2,1)} fusion(bf16[2,64,8,32]{3,0,2,1:T(2,128)(2,1)} %copy.164, bf16[2,32,8,64]{1,0,2,3:T(2,128)(2,1)} %copy.149), kind=kOutput, calls=%fused_computation.2 | convolution fusion | flops 2621440 | bytes 1179648 | tf_op jit(solution)/shard_map/mnhp,mphd->nphd/dot_general | solution.py:149
  126.9 4.9 %copy.168 = bf16[32,64,256]{2,1,0:T(8,128)(2,1)} copy(bf16[32,64,256]{0,2,1:T(8,128)(2,1)} %bitcast.185) | data formatting | bytes 2097152 | tf_op jit(solution)/shard_map/reshape | solution.py:156
  131.7 3.1 pad_maximum_fusion
  134.8 7.8 %copy.156 = bf16[32,64,8,32]{3,0,2,1:T(8,128)(2,1)} copy(bf16[32,64,8,32]{1,3,2,0:T(8,128)(2,1)} %bitcast.183) | data formatting | bytes 2097152 | tf_op jit(solution)/shard_map/reshape | solution.py:39
  142.6 6.8 %copy.148 = bf16[32,64,8,32]{3,0,2,1:T(8,128)(2,1)} copy(bf16[32,64,8,32]{1,3,2,0:T(8,128)(2,1)S(1)} %bitcast.181) | data formatting | bytes 2097152 | tf_op jit(solution)/shard_map/reshape | solution.py:39
  149.5 3.5 fusion.116
  153.9 3.4 fusion.1
  157.6 179.7 %reduce-scatter.2.cloned.1.call-done = bf16[2,64,512]{2,1,0:T(8,128)(2,1)} async-done(((bf16[32,64,512]{2,1,0:T(8,128)(2,1)}), bf16[2,64,512]{2,1,0:T(8,128)(2,1)}) %reduce-scatter.2.cloned.1.call-update) | async-done | bytes 131088 | tf_op jit(solution)/shard_map/reduce_scatter | solution.py:152
  340.4 6.3 %collective-permute-start = (bf16[2,4,1,256]{3,2,1,0:T(2,128)(2,1)S(1)}, bf16[2,4,1,256]{3,2,1,0:T(2,128)(2,1)S(1)}, u32[]{:S(2)}, u32[]{:S(2)}) collective-permute-start(bf16[2,4,1,256]{3,2,1,0:T(2,128)(2,1)S(1)} %get-tuple-element.16), channel_id=1, source_target_pairs={{0,1},{1,2},{2,3},{3,0},{4,5},{5,6},{6,7},{7,4},{8,9},{9,10},{10,1... | collective-permute-start | bytes 12296 | tf_op jit(solution)/shard_map/ppermute | solution.py:19
  347.6 2.2 collective-permute-done.1
  349.8 3.1 collective-permute-start.2
  352.9 1.3 collective-permute-start.3
  354.4 3.1 collective-permute-done.3
  (93 shorter events, 13.6 us)
Async XLA Ops:
  7.2 28.8 %copy-start = (bf16[256,256]{1,0:T(8,128)(2,1)S(1)}, bf16[256,256]{1,0:T(8,128)(2,1)}, u32[]{:S(2)}) copy-start(bf16[256,256]{1,0:T(8,128)(2,1)} %param.9) | copy-start | bytes 393220
  7.2 17.4 %copy-start.5 = (bf16[2,4,16,256]{3,2,1,0:T(8,128)(2,1)S(1)}, bf16[2,4,16,256]{3,2,1,0:T(8,128)(2,1)}, u32[]{:S(2)}) copy-start(bf16[2,4,16,256]{3,2,1,0:T(8,128)(2,1)} %param.11) | copy-start | bytes 196612
  7.2 17.4 %copy-start.2 = (bf16[3,3,256,256]{3,2,1,0:T(8,128)(2,1)S(1)}, bf16[3,3,256,256]{3,2,1,0:T(8,128)(2,1)}, u32[]{:S(2)}) copy-start(bf16[3,3,256,256]{3,2,1,0:T(8,128)(2,1)} %param.10) | copy-start | bytes 3538948
  8.1 20.1 %collective-permute-start.4 = (bf16[2,4,1,256]{3,2,1,0:T(2,128)(2,1)S(1)}, bf16[2,4,1,256]{3,2,1,0:T(2,128)(2,1)S(1)}, u32[]{:S(2)}, u32[]{:S(2)}) collective-permute-start(bf16[2,4,1,256]{3,2,1,0:T(2,128)(2,1)S(1)} %get-tuple-element.18), channel_id=1, source_target_pairs={{0,1},{1,2},{2,3},{3,0},{4,5},{5,6},{6,7},{7,4},{8,9},{9,10},{10,1... | collective-permute-start | bytes 12296 | tf_op jit(solution)/shard_map/ppermute | solution.py:19
  10.9 17.4 %collective-permute-start.5 = (bf16[2,4,1,256]{3,2,1,0:T(2,128)(2,1)S(1)}, bf16[2,4,1,256]{3,2,1,0:T(2,128)(2,1)S(1)}, u32[]{:S(2)}, u32[]{:S(2)}) collective-permute-start(bf16[2,4,1,256]{3,2,1,0:T(2,128)(2,1)S(1)} %get-tuple-element.19), channel_id=1, source_target_pairs={{1,0},{2,1},{3,2},{0,3},{5,4},{6,5},{7,6},{4,7},{9,8},{10,9},{11,1... | collective-permute-start | bytes 12296 | tf_op jit(solution)/shard_map/ppermute | solution.py:22
  14.5 36.7 %all-to-all-start = ((bf16[16,2,64,256]{3,2,1,0:T(8,128)(2,1)}), bf16[16,2,64,256]{3,2,1,0:T(8,128)(2,1)S(1)}, u32[]{:S(2)}, u32[]{:S(2)}) async-start(bf16[16,2,64,256]{3,2,1,0:T(8,128)(2,1)} %stack.2), calls=%async_computation | async-start | bytes 2097152 | tf_op jit(solution)/shard_map/all_to_all | solution.py:89
  24.6 312.7 %reduce-scatter.2.cloned.1.call-start = ((), (), s32[]{:S(2)}) async-start(), calls=%async_computation.2 | async-start | bytes 2228224 | tf_op jit(solution)/shard_map/reduce_scatter | solution.py:152
  26.0 9.3 %copy-start.3 = (f32[2,64,256]{1,2,0:T(8,128)}, f32[2,64,256]{1,2,0:T(8,128)S(1)}, u32[]{:S(2)}) copy-start(f32[2,64,256]{1,2,0:T(8,128)S(1)} %copy.142) | copy-start | bytes 393220
  28.3 5.5 %collective-permute-start.6 = (bf16[2,1,18,256]{3,2,1,0:T(8,128)(2,1)S(1)}, bf16[2,1,18,256]{3,2,1,0:T(8,128)(2,1)S(1)}, u32[]{:S(2)}, u32[]{:S(2)}) collective-permute-start(bf16[2,1,18,256]{3,2,1,0:T(8,128)(2,1)S(1)} %get-tuple-element.14), channel_id=1, source_target_pairs={{4,0},{8,4},{12,8},{5,1},{9,5},{13,9},{6,2},{10,6},{14,10},{7,3},{... | collective-permute-start | bytes 55304 | tf_op jit(solution)/shard_map/ppermute | solution.py:22
  29.6 4.9 %collective-permute-start.7 = (bf16[2,1,18,256]{3,2,1,0:T(8,128)(2,1)S(1)}, bf16[2,1,18,256]{3,2,1,0:T(8,128)(2,1)S(1)}, u32[]{:S(2)}, u32[]{:S(2)}) collective-permute-start(bf16[2,1,18,256]{3,2,1,0:T(8,128)(2,1)S(1)} %get-tuple-element.15), channel_id=1, source_target_pairs={{0,4},{4,8},{8,12},{1,5},{5,9},{9,13},{2,6},{6,10},{10,14},{3,7},{... | collective-permute-start | bytes 55304 | tf_op jit(solution)/shard_map/ppermute | solution.py:19
  52.9 1.7 copy-start.1
  149.5 3.8 %copy-start.4 = (f32[2,64,256]{1,2,0:T(8,128)S(1)}, f32[2,64,256]{1,2,0:T(8,128)}, u32[]{:S(2)}) copy-start(f32[2,64,256]{1,2,0:T(8,128)} %copy-done.3) | copy-start | bytes 393220
  152.9 1.0 copy-start.6
  157.3 182.5 %copy-start.7 = (bf16[2,4,16,256]{3,2,1,0:T(8,128)(2,1)S(1)}, bf16[2,4,16,256]{3,2,1,0:T(8,128)(2,1)}, u32[]{:S(2)}) copy-start(bf16[2,4,16,256]{3,2,1,0:T(8,128)(2,1)} %param.6) | copy-start | bytes 196612
  157.3 182.5 %copy-start.8 = (bf16[256,768]{1,0:T(8,128)(2,1)S(1)}, bf16[256,768]{1,0:T(8,128)(2,1)}, u32[]{:S(2)}) copy-start(bf16[256,768]{1,0:T(8,128)(2,1)} %param.8) | copy-start | bytes 1179652
  157.3 182.5 %copy-start.10 = (f32[256]{0:T(256)S(1)}, f32[256]{0:T(256)}, u32[]{:S(2)}) copy-start(f32[256]{0:T(256)} %param.7) | copy-start | bytes 3076
  337.3 1.6 copy-start.9
  337.3 2.5 slice-start
  340.4 7.2 %collective-permute-start = (bf16[2,4,1,256]{3,2,1,0:T(2,128)(2,1)S(1)}, bf16[2,4,1,256]{3,2,1,0:T(2,128)(2,1)S(1)}, u32[]{:S(2)}, u32[]{:S(2)}) collective-permute-start(bf16[2,4,1,256]{3,2,1,0:T(2,128)(2,1)S(1)} %get-tuple-element.16), channel_id=1, source_target_pairs={{0,1},{1,2},{2,3},{3,0},{4,5},{5,6},{6,7},{7,4},{8,9},{9,10},{10,1... | collective-permute-start | bytes 12296 | tf_op jit(solution)/shard_map/ppermute | solution.py:19
  346.7 3.1 collective-permute-start.1
  349.8 4.6 %collective-permute-start.2 = (bf16[2,1,18,256]{3,2,1,0:T(8,128)(2,1)S(1)}, bf16[2,1,18,256]{3,2,1,0:T(8,128)(2,1)S(1)}, u32[]{:S(2)}, u32[]{:S(2)}) collective-permute-start(bf16[2,1,18,256]{3,2,1,0:T(8,128)(2,1)S(1)} %get-tuple-element.10), channel_id=1, source_target_pairs={{0,4},{4,8},{8,12},{1,5},{5,9},{9,13},{2,6},{6,10},{10,14},{3,7},{... | collective-permute-start | bytes 55304 | tf_op jit(solution)/shard_map/ppermute | solution.py:19
  352.9 4.6 %collective-permute-start.3 = (bf16[2,1,18,256]{3,2,1,0:T(8,128)(2,1)S(1)}, bf16[2,1,18,256]{3,2,1,0:T(8,128)(2,1)S(1)}, u32[]{:S(2)}, u32[]{:S(2)}) collective-permute-start(bf16[2,1,18,256]{3,2,1,0:T(8,128)(2,1)S(1)} %get-tuple-element.11), channel_id=1, source_target_pairs={{4,0},{8,4},{12,8},{5,1},{9,5},{13,9},{6,2},{10,6},{14,10},{7,3},{... | collective-permute-start | bytes 55304 | tf_op jit(solution)/shard_map/ppermute | solution.py:22
Sparse Core Ops, SparseCore 0:
  135.0 202.2 reduce-scatter.1
